TPU v7x, 32 devices: a whole 2x2x4 slice. The times are simulated.
32 devices in a mesh: gx: 8 (over z, y), gy: 4 (over x, core).
Axes of the slice: x: 2, y: 2, z: 4, core: 2. Of those that a mesh axis runs over, the one named last changes fastest.
Arguments:
- psi: float32 [2, 256, 16, 1024], P(None, 'gx', None, 'gy'), may hold values from -6 to 6
- potential: float32 [256, 16, 1024], P('gx', None, 'gy'), may hold values from 0 to 4
Outputs:
- psi_half: float32 [2, 256, 16, 1024], P(None, 'gx', None, 'gy')
All inputs are finite; a program needn't handle non-finite values.
Results may differ from a plain program's by a relative error of at most 0.00005.
Values sent between devices are 32-bit elements; how exact they have to be, the bound alone decides.
A program may use at most 64 MiB of HBM per device.

v0:
```python
import jax
import jax.numpy as jnp
import numpy as np
from jax import lax
from jax.sharding import PartitionSpec as P

RYZ = 2


def with_halo(value, sides, width):
    for axis, dim in sides:
        peers, length = (lax.axis_size(axis), value.shape[dim])
        up = [(i, (i + 1) % peers) for i in range(peers - 1)]
        down = [(j, i) for i, j in up]
        last = lax.slice_in_dim(value, length - width, length, axis=dim)
        first = lax.slice_in_dim(value, 0, width, axis=dim)
        before = lax.ppermute(last, axis, up)
        after = lax.ppermute(first, axis, down)
        value = jnp.concatenate([before, value, after], axis=dim)
    return value


def cmul(left, right):
    return jnp.stack(
        [left[0] * right[0] - left[1] * right[1], left[0] * right[1] + left[1] * right[0]]
    )


def cinv(value):
    denom = value[0] * value[0] + value[1] * value[1]
    return jnp.stack([value[0] / denom, -value[1] / denom])


def local_inverse(cells):
    coef = 256.0 * cells * cells
    identity = np.eye(cells)
    cp_re_list = []
    cp_im_list = []
    dp_re_list = []
    dp_im_list = []
    cp_re = 0.0
    cp_im = 0.0
    dp_re = np.zeros(cells)
    dp_im = np.zeros(cells)
    for index in range(cells):
        piv_re = 1.0 - coef * cp_im
        piv_im = 2.0 * coef + coef * cp_re
        denom = piv_re * piv_re + piv_im * piv_im
        cp_re = -coef * piv_im / denom
        cp_im = -coef * piv_re / denom
        num_re = identity[index] - coef * dp_im
        num_im = coef * dp_re
        dp_re = (num_re * piv_re + num_im * piv_im) / denom
        dp_im = (num_im * piv_re - num_re * piv_im) / denom
        cp_re_list.append(cp_re)
        cp_im_list.append(cp_im)
        dp_re_list.append(dp_re)
        dp_im_list.append(dp_im)
    inv_re = np.zeros((cells, cells))
    inv_im = np.zeros((cells, cells))
    later_re = np.zeros(cells)
    later_im = np.zeros(cells)
    for index in range(cells - 1, -1, -1):
        next_re = dp_re_list[index] - (cp_re_list[index] * later_re - cp_im_list[index] * later_im)
        next_im = dp_im_list[index] - (cp_re_list[index] * later_im + cp_im_list[index] * later_re)
        later_re, later_im = (next_re, next_im)
        inv_re[index] = later_re
        inv_im[index] = later_im
    return (inv_re, inv_im, coef)


def shards(psi, potential):
    cells = psi.shape[1]
    count = lax.axis_size("gx")
    place = lax.axis_index("gx")
    inv_re, inv_im, coef = local_inverse(cells)
    upper_half = np.concatenate([inv_re, -inv_im], axis=1)
    lower_half = np.concatenate([inv_im, inv_re], axis=1)
    big = np.concatenate([upper_half, lower_half], axis=0).astype(np.float32)
    g_vec = jnp.asarray(np.stack([-coef * inv_im[:, 0], coef * inv_re[:, 0]]).astype(np.float32))
    h_vec = jnp.asarray(
        np.stack([-coef * inv_im[:, cells - 1], coef * inv_re[:, cells - 1]]).astype(np.float32)
    )
    s_val = g_vec[:, 0]
    t_val = g_vec[:, cells - 1]
    real_part, imag_part = (psi[0], psi[1])
    theta = 0.5 * (potential + real_part * real_part + imag_part * imag_part)
    cosine, sine = (jnp.cos(theta), jnp.sin(theta))
    turned = jnp.stack(
        [real_part * cosine + imag_part * sine, imag_part * cosine - real_part * sine]
    )
    padded = with_halo(turned, (("gy", 3),), 1)
    lap_y = padded[:, :, :, 2:] + padded[:, :, :, :-2] - 2.0 * turned
    z_padded = jnp.pad(turned, ((0, 0), (0, 0), (1, 1), (0, 0)))
    lap_z = z_padded[:, :, 2:] + z_padded[:, :, :-2] - 2.0 * turned
    side = RYZ * (lap_y + lap_z)
    rhs = jnp.stack([2.0 * turned[0] - side[1], 2.0 * turned[1] + side[0]])
    planes = rhs.shape[2]
    lines = rhs.shape[3]
    flat = rhs.reshape(2 * cells, planes * lines)
    local = jnp.dot(jnp.asarray(big), flat, precision=lax.Precision.HIGHEST).reshape(
        2, cells, planes, lines
    )
    first_val = local[:, 0]
    last_val = local[:, cells - 1]

    def advance(alpha, unused):
        q_val = cinv(
            jnp.stack(
                [
                    1.0 - (s_val[0] * alpha[0] - s_val[1] * alpha[1]),
                    -(s_val[0] * alpha[1] + s_val[1] * alpha[0]),
                ]
            )
        )
        aq_val = cmul(alpha, q_val)
        c_val = cmul(t_val, jnp.stack([1.0, 0.0]) + cmul(aq_val, s_val))
        mu_val = cmul(q_val, t_val)
        new_alpha = s_val + cmul(cmul(t_val, t_val), aq_val)
        return (new_alpha, (alpha, q_val, c_val, mu_val))

    unused, tables = lax.scan(advance, jnp.zeros((2,), jnp.float32), None, length=count)
    alphas, q_vals, c_vals, mu_vals = tables
    alpha_here = lax.dynamic_index_in_dim(alphas, place, 0, keepdims=False)
    q_here = lax.dynamic_index_in_dim(q_vals, place, 0, keepdims=False)
    mu_here = lax.dynamic_index_in_dim(mu_vals, place, 0, keepdims=False)
    fwd_term = last_val + cmul(cmul(t_val, cmul(alpha_here, q_here)), first_val)
    positions = jnp.arange(count, dtype=jnp.int32)

    def fwd_row(row, item):
        factor, index = item
        onehot = jnp.stack(
            [(positions == index).astype(jnp.float32), jnp.zeros((count,), jnp.float32)]
        )
        return (cmul(factor, row) + onehot, row)

    unused, fwd_rows = lax.scan(fwd_row, jnp.zeros((2, count), jnp.float32), (c_vals, positions))
    fwd_weights = lax.dynamic_index_in_dim(fwd_rows, place, 0, keepdims=False)
    piece = lax.all_gather(fwd_term[None], "gx", axis=0, tiled=True)
    weights = lax.slice_in_dim(fwd_weights, 0, piece.shape[0], axis=1)
    part_re = jnp.einsum(
        "k,kzy->zy", weights[0], piece[:, 0], precision=lax.Precision.HIGHEST
    ) - jnp.einsum("k,kzy->zy", weights[1], piece[:, 1], precision=lax.Precision.HIGHEST)
    part_im = jnp.einsum(
        "k,kzy->zy", weights[0], piece[:, 1], precision=lax.Precision.HIGHEST
    ) + jnp.einsum("k,kzy->zy", weights[1], piece[:, 0], precision=lax.Precision.HIGHEST)
    beta_prev = jnp.zeros_like(fwd_term) + jnp.stack([part_re, part_im])
    nu_here = cmul(q_here, first_val + cmul(s_val, beta_prev))

    def back_row(row, item):
        factor, index = item
        onehot = jnp.stack(
            [(positions == index).astype(jnp.float32), jnp.zeros((count,), jnp.float32)]
        )
        return (cmul(factor, row) + onehot, row)

    unused, back_rows = lax.scan(
        back_row, jnp.zeros((2, count), jnp.float32), (mu_vals, positions), reverse=True
    )
    back_weights = lax.dynamic_index_in_dim(back_rows, place, 0, keepdims=False)
    piece = lax.all_gather(nu_here[None], "gx", axis=0, tiled=True)
    weights = lax.slice_in_dim(back_weights, 0, piece.shape[0], axis=1)
    part_re = jnp.einsum(
        "k,kzy->zy", weights[0], piece[:, 0], precision=lax.Precision.HIGHEST
    ) - jnp.einsum("k,kzy->zy", weights[1], piece[:, 1], precision=lax.Precision.HIGHEST)
    part_im = jnp.einsum(
        "k,kzy->zy", weights[0], piece[:, 1], precision=lax.Precision.HIGHEST
    ) + jnp.einsum("k,kzy->zy", weights[1], piece[:, 0], precision=lax.Precision.HIGHEST)
    next_first = jnp.zeros_like(nu_here) + jnp.stack([part_re, part_im])
    first_here = cmul(mu_here, next_first) + nu_here
    edge_prev = cmul(alpha_here, first_here) + beta_prev
    from_left = cmul(g_vec[:, :, None, None], edge_prev[:, None])
    from_right = cmul(h_vec[:, :, None, None], next_first[:, None])
    return local + from_left + from_right - turned


def solution(mesh):
    return jax.shard_map(
        shards,
        mesh=mesh,
        in_specs=(P(None, "gx", None, "gy"), P("gx", None, "gy")),
        out_specs=P(None, "gx", None, "gy"),
        check_vma=False,
    )
```

profile of v0, /device:TPU:0, one launch (start us, length us, event | category | flops | bytes accessed | tf_op | source)
XLA Modules:
  0.0 309.6 jit_solution(17856614827695865240)
XLA Ops:
  0.0 3.6 %fusion.18 = (f32[32,16,256]{2,1,0:T(8,128)S(1)}, f32[32,16,256]{2,1,0:T(8,128)S(1)}) fusion(f32[2,32,16,256]{3,2,1,0:T(8,128)} %param.11, f32[32,16,256]{2,1,0:T(8,128)} %param.12), kind=kLoop, calls=%fused_computation.56 | loop fusion | flops 1441792 | bytes 2621440 | tf_op jit(solution)/shard_map/add | solution.py:90
  3.9 1.3 collective-permute-start
  5.2 3.8 %collective-permute-start.1 = (f32[2,32,16,1]{3,2,1,0:T(8,128)S(1)}, f32[2,32,16,1]{3,2,1,0:T(8,128)}, u32[]{:S(2)}, u32[]{:S(2)}) collective-permute-start(f32[2,32,16,1]{3,2,1,0:T(8,128)S(1)} %get-tuple-element.456), channel_id=1, source_target_pairs={{0,1},{1,2},{2,3},{4,5},{5,6},{6,7},{8,9},{9,10},{10,11},{12,13},{... | collective-permute-start | bytes 12296 | tf_op jit(solution)/shard_map/ppermute | solution.py:17
  9.7 162.3 %while.56 = (s32[]{:T(128)}, f32[2]{0:T(128)S(1)}, f32[8,2]{1,0:T(8,128)S(1)}, f32[8,2]{1,0:T(8,128)S(1)}, f32[8,2]{1,0:T(8,128)S(1)}, /*index=5*/f32[8,2]{1,0:T...) while((s32[]{:T(128)}, f32[2]{0:T(128)S(1)}, ...), condition=%wide.region_1.2_spmd.clone.clone, body=%wide.region_0.1_spmd.clone.clone.sunk | while | flops 63 | bytes 928 | solution.py:122
  173.8 26.4 %while.55 = (s32[]{:T(128)}, f32[2,8]{1,0:T(2,128)S(1)}, f32[8,2,8]{2,1,0:T(2,128)S(1)}, f32[8,2]{1,0:T(8,128)S(1)}, s32[8]{0:T(128)S(1)}, /*index=5*/s32[]{:T(128)}, s32[]{:T(128)}) while((s32[]{:T(128)}, f32[2,8]{1,0:T(2,128)S(1)}, f32[8,2,8]{2,1,0:T(2,128)S(1)}, f32[8,2]{1,0:T(8,128)S(1)}, s32[8]{0:T(128)S(1)}, ...), condition=%wide.region_5.6_spmd.clone.clone, body=%wide.region_4.5_spmd.clone.clone.sunk | while | flops 123 | bytes 3535 | solution.py:137
  175.8 1.3 multiply_subtract_fusion.10
  182.4 1.3 multiply_subtract_fusion.10
  185.7 1.3 multiply_subtract_fusion.10
  192.3 1.3 multiply_subtract_fusion.10
  199.0 1.3 multiply_subtract_fusion.10
  200.3 26.6 %while.54 = (s32[]{:T(128)}, f32[2,8]{1,0:T(2,128)S(1)}, f32[8,2,8]{2,1,0:T(2,128)S(1)}, f32[8,2]{1,0:T(8,128)S(1)}, s32[8]{0:T(128)S(1)}, /*index=5*/s32[]{:T(128)}, s32[]{:T(128)}, s32[]{:T(128)}) while((s32[]{:T(128)}, f32[2,8]{1,0:T(2,128)S(1)}, f32[8,2,8]{2,1,0:T(2,128)S(1)}, f32[8,2]{1,0:T(8,128)S(1)}, ...), condition=%wide.region_3.4_spmd.clone.clone, body=%wide.region_2.3_spmd.clone.clone.sunk | while | flops 124 | bytes 3555 | solution.py:157
  202.3 1.3 multiply_subtract_fusion.9
  205.6 1.3 multiply_subtract_fusion.9
  208.9 1.3 multiply_subtract_fusion.9
  212.2 1.3 multiply_subtract_fusion.9
  215.6 1.3 multiply_subtract_fusion.9
  218.9 1.3 multiply_subtract_fusion.9
  222.2 1.3 multiply_subtract_fusion.9
  225.5 1.3 multiply_subtract_fusion.9
  232.1 1.9 fusion.5
  236.5 32.7 %all_gather.6 = f32[8,2,16,256]{3,2,1,0:T(8,128)S(1)} all-gather(f32[1,2,16,256]{3,2,1,0:T(8,128)S(1)} %fusion.37), channel_id=1, replica_groups=mesh['gx'=8,'gy'=4] {'gx'}, dimensions={0}, use_global_device_ids=true | all-gather | bytes 294912 | tf_op jit(solution)/shard_map/all_gather | solution.py:139
  271.9 30.7 %all-gather = f32[16,16,256]{2,1,0:T(8,128)S(1)} all-gather(f32[2,16,256]{2,1,0:T(8,128)S(1)} %pad_maximum_fusion.6), channel_id=2, replica_groups=mesh['gx'=8,'gy'=4] {'gx'}, dimensions={0}, use_global_device_ids=true | all-gather | bytes 294912 | tf_op jit(solution)/shard_map/all_gather | solution.py:161
  306.4 1.4 multiply_subtract_fusion.4
  308.2 1.5 fusion.9
  (277 shorter events, 65.6 us)
Async XLA Ops:
  3.9 228.2 %collective-permute-start = (f32[2,32,16,1]{3,2,1,0:T(8,128)S(1)}, f32[2,32,16,1]{3,2,1,0:T(8,128)}, u32[]{:S(2)}, u32[]{:S(2)}) collective-permute-start(f32[2,32,16,1]{3,2,1,0:T(8,128)S(1)} %get-tuple-element.455), channel_id=1, source_target_pairs={{1,0},{2,1},{3,2},{5,4},{6,5},{7,6},{9,8},{10,9},{11,10},{13,12},{... | collective-permute-start | bytes 12296 | tf_op jit(solution)/shard_map/ppermute | solution.py:18
  5.2 226.9 %collective-permute-start.1 = (f32[2,32,16,1]{3,2,1,0:T(8,128)S(1)}, f32[2,32,16,1]{3,2,1,0:T(8,128)}, u32[]{:S(2)}, u32[]{:S(2)}) collective-permute-start(f32[2,32,16,1]{3,2,1,0:T(8,128)S(1)} %get-tuple-element.456), channel_id=1, source_target_pairs={{0,1},{1,2},{2,3},{4,5},{5,6},{6,7},{8,9},{9,10},{10,11},{12,13},{... | collective-permute-start | bytes 12296 | tf_op jit(solution)/shard_map/ppermute | solution.py:17
  9.0 0.7 copy-start
  9.0 0.7 copy-start.1
  9.0 0.7 copy-start.3
  234.4 0.8 copy-start.2
  270.6 37.2 %copy-start.6 = (f32[32]{0:T(128)S(1)}, f32[32]{0:T(128)}, u32[]{:S(2)}) copy-start(f32[32]{0:T(128)} %constant.154) | copy-start | bytes 388
  270.6 37.2 %copy-start.7 = (f32[32]{0:T(128)S(1)}, f32[32]{0:T(128)}, u32[]{:S(2)}) copy-start(f32[32]{0:T(128)} %constant.152) | copy-start | bytes 388
  302.9 5.0 %copy-start.4 = (f32[32]{0:T(128)S(1)}, f32[32]{0:T(128)}, u32[]{:S(2)}) copy-start(f32[32]{0:T(128)} %constant.150) | copy-start | bytes 388
  303.0 5.0 %copy-start.5 = (f32[32]{0:T(128)S(1)}, f32[32]{0:T(128)}, u32[]{:S(2)}) copy-start(f32[32]{0:T(128)} %constant.131) | copy-start | bytes 388
where the time goes:
time: 313 us; the launch traced here: 310 us
  loops' own time  144 us (46%)
  blocking collectives  63.5 us (20%)
  other arithmetic  47.9 us (15%)
  local copies, waits for them, and re-layouts  39.6 us (13%)
  between operations  5.62 us (2%)
  starting transfers between devices  5.13 us (2%)
  matrix products  3.47 us (1%)
    another operation x1, loops' own time, shards(): lax.scan(advance, jnp.zeros((2,), jnp.float32), None, length=count)  144 us
    all_gather x1, blocking collectives, shards(): piece = lax.all_gather(fwd_term[None], 'gx', axis=0, tiled=True)  32.7 us
    all_gather x1, blocking collectives, shards(): piece = lax.all_gather(nu_here[None], 'gx', axis=0, tiled=True)  30.7 us
    sub x21, other arithmetic, cmul(): left[0] * right[0] - left[1] * right[1]  23.7 us
    slice x18, local copies, waits for them, and re-layouts, cmul(): left[0] * right[0] - left[1] * right[1]  11.3 us
    dynamic_slice x32, local copies, waits for them, and re-layouts, shards(): lax.scan(fwd_row, jnp.zeros((2, count), jnp.float32), (c_vals, positions))  10.4 us
  transfers between devices with their start and end apart: 2, of which 0 were waited for; matrix products, arithmetic and copies ran while one was open for 23% of the time, Pallas kernels for 0%

commit v1 on v0

--- a/solution.py
+++ b/solution.py
@@ -136,7 +136,14 @@
 
     unused, fwd_rows = lax.scan(fwd_row, jnp.zeros((2, count), jnp.float32), (c_vals, positions))
     fwd_weights = lax.dynamic_index_in_dim(fwd_rows, place, 0, keepdims=False)
-    piece = lax.all_gather(fwd_term[None], "gx", axis=0, tiled=True)
+    part = fwd_term[None]
+    size = lax.axis_size("gx")
+    moving, parts = (part, [part])
+    for _ in range(size - 1):
+        moving = lax.ppermute(moving, "gx", [(i_2, (i_2 + 1) % size) for i_2 in range(size)])
+        parts.insert(0, moving)
+    merged = jnp.concatenate(parts, axis=0)
+    piece = jnp.roll(merged, (lax.axis_index("gx") + 1) * part.shape[0], axis=0)
     weights = lax.slice_in_dim(fwd_weights, 0, piece.shape[0], axis=1)
     part_re = jnp.einsum(
         "k,kzy->zy", weights[0], piece[:, 0], precision=lax.Precision.HIGHEST

time: 313 us -> 303 us (0.968)
  blocking collectives: 63.5 us -> 30.7 us
  waiting for transfers between devices: 0.01 us -> 30.8 us
  loops' own time: 144 us -> 138 us
  other arithmetic: 47.9 us -> 44.1 us
  starting transfers between devices: 5.13 us -> 8.32 us
    all_gather x1 -> x0, blocking collectives: 32.7 us -> none  [shards(): piece = lax.all_gather(fwd_term[None], 'gx', axis=0, tiled=True)]
    ppermute x0 -> x7, waiting for transfers between devices: none -> 30.8 us  [shards(): lax.ppermute(moving, 'gx', [(i_2, (i_2 + 1) % size) for i_2 in range(size)])]
    another operation x1, loops' own time: 144 us -> 137 us  [shards(): lax.scan(advance, jnp.zeros((2,), jnp.float32), None, length=count)]
    ppermute x0 -> x7, starting transfers between devices: none -> 3.18 us  [shards(): lax.ppermute(moving, 'gx', [(i_2, (i_2 + 1) % size) for i_2 in range(size)])]
  transfers between devices with their start and end apart: 2 -> 9, of which waited for: 0 -> 5; matrix products, arithmetic and copies ran while one was open for 23% -> 23% of each run, Pallas kernels for 0% -> 0%
where the time goes in v1:
time: 303 us; the launch traced here: 300 us
  loops' own time  138 us (46%)
  other arithmetic  44.1 us (15%)
  local copies, waits for them, and re-layouts  38.8 us (13%)
  waiting for transfers between devices  30.8 us (10%)
  blocking collectives  30.7 us (10%)
  starting transfers between devices  8.32 us (3%)
  between operations  5.62 us (2%)
  matrix products  3.46 us (1%)
    another operation x1, loops' own time, shards(): lax.scan(advance, jnp.zeros((2,), jnp.float32), None, length=count)  137 us
    ppermute x7, waiting for transfers between devices, shards(): lax.ppermute(moving, 'gx', [(i_2, (i_2 + 1) % size) for i_2 in range(size)])  30.8 us
    all_gather x1, blocking collectives, shards(): piece = lax.all_gather(nu_here[None], 'gx', axis=0, tiled=True)  30.7 us
    sub x21, other arithmetic, cmul(): left[0] * right[0] - left[1] * right[1]  21.8 us
    slice x18, local copies, waits for them, and re-layouts, cmul(): left[0] * right[0] - left[1] * right[1]  11.6 us
    dynamic_slice x32, local copies, waits for them, and re-layouts, shards(): lax.scan(fwd_row, jnp.zeros((2, count), jnp.float32), (c_vals, positions))  9.06 us
  transfers between devices with their start and end apart: 9, of which 5 were waited for; matrix products, arithmetic and copies ran while one was open for 23% of the time, Pallas kernels for 0%

profile of v1, /device:TPU:0, one launch (start us, length us, event | category | flops | bytes accessed | tf_op | source)
XLA Modules:
  0.0 300.0 jit_solution(10008975815166851012)
XLA Ops:
  0.0 3.6 %fusion.18 = (f32[32,16,256]{2,1,0:T(8,128)S(1)}, f32[32,16,256]{2,1,0:T(8,128)S(1)}) fusion(f32[2,32,16,256]{3,2,1,0:T(8,128)} %param.11, f32[32,16,256]{2,1,0:T(8,128)} %param.12), kind=kLoop, calls=%fused_computation.56 | loop fusion | flops 1441792 | bytes 2621440 | tf_op jit(solution)/shard_map/add | solution.py:90
  3.9 1.3 collective-permute-start
  5.2 3.8 %collective-permute-start.1 = (f32[2,32,16,1]{3,2,1,0:T(8,128)S(1)}, f32[2,32,16,1]{3,2,1,0:T(8,128)}, u32[]{:S(2)}, u32[]{:S(2)}) collective-permute-start(f32[2,32,16,1]{3,2,1,0:T(8,128)S(1)} %get-tuple-element.456), channel_id=1, source_target_pairs={{0,1},{1,2},{2,3},{4,5},{5,6},{6,7},{8,9},{9,10},{10,11},{12,13},{... | collective-permute-start | bytes 12296 | tf_op jit(solution)/shard_map/ppermute | solution.py:17
  9.7 156.3 %while.56 = (s32[]{:T(128)}, f32[2]{0:T(128)S(1)}, f32[8,2]{1,0:T(8,128)S(1)}, f32[8,2]{1,0:T(8,128)S(1)}, f32[8,2]{1,0:T(8,128)S(1)}, /*index=5*/f32[8,2]{1,0:T...) while((s32[]{:T(128)}, f32[2]{0:T(128)S(1)}, ...), condition=%wide.region_1.2_spmd.clone.clone, body=%wide.region_0.1_spmd.clone.clone.sunk | while | flops 63 | bytes 928 | solution.py:122
  172.3 1.9 fusion.5
  176.7 3.1 %collective-permute-start.2 = (f32[1,2,16,256]{3,2,1,0:T(8,128)S(1)}, f32[1,2,16,256]{3,2,1,0:T(8,128)S(1)}, u32[]{:S(2)}, u32[]{:S(2)}) collective-permute-start(f32[1,2,16,256]{3,2,1,0:T(8,128)S(1)} %fusion.37), channel_id=1, source_target_pairs={{0,4},{4,8},{8,12},{12,16},{16,20},{20,24},{24,28},{28,0},{1,5},{5... | collective-permute-start | bytes 98312 | tf_op jit(solution)/shard_map/ppermute | solution.py:143
  179.8 4.9 %collective-permute-done.2 = f32[1,2,16,256]{3,2,1,0:T(8,128)S(1)} collective-permute-done((f32[1,2,16,256]{3,2,1,0:T(8,128)S(1)}, f32[1,2,16,256]{3,2,1,0:T(8,128)S(1)}, u32[]{:S(2)}, u32[]{:S(2)}) %collective-permute-start.2) | collective-permute-done | bytes 32800 | tf_op jit(solution)/shard_map/ppermute | solution.py:143
  184.7 6.6 %collective-permute-done.3 = f32[1,2,16,256]{3,2,1,0:T(8,128)S(1)} collective-permute-done((f32[1,2,16,256]{3,2,1,0:T(8,128)S(1)}, f32[1,2,16,256]{3,2,1,0:T(8,128)S(1)}, u32[]{:S(2)}, u32[]{:S(2)}) %collective-permute-start.3) | collective-permute-done | bytes 32800 | tf_op jit(solution)/shard_map/ppermute | solution.py:143
  191.4 6.6 %collective-permute-done.4 = f32[1,2,16,256]{3,2,1,0:T(8,128)S(1)} collective-permute-done((f32[1,2,16,256]{3,2,1,0:T(8,128)S(1)}, f32[1,2,16,256]{3,2,1,0:T(8,128)S(1)}, u32[]{:S(2)}, u32[]{:S(2)}) %collective-permute-start.4) | collective-permute-done | bytes 32800 | tf_op jit(solution)/shard_map/ppermute | solution.py:143
  198.0 24.1 %while.54 = (s32[]{:T(128)}, f32[2,8]{1,0:T(2,128)S(1)}, f32[8,2,8]{2,1,0:T(2,128)S(1)}, f32[8,2]{1,0:T(8,128)S(1)}, s32[8]{0:T(128)S(1)}, /*index=5*/s32[]{:T(128)}, s32[]{:T(128)}, s32[]{:T(128)}) while((s32[]{:T(128)}, f32[2,8]{1,0:T(2,128)S(1)}, f32[8,2,8]{2,1,0:T(2,128)S(1)}, f32[8,2]{1,0:T(8,128)S(1)}, ...), condition=%wide.region_3.4_spmd.clone.clone, body=%wide.region_2.3_spmd.clone.clone.sunk | while | flops 124 | bytes 3555 | solution.py:164
  199.8 1.2 multiply_subtract_fusion.9
  202.8 1.2 multiply_subtract_fusion.9
  205.8 1.2 multiply_subtract_fusion.9
  208.8 1.2 multiply_subtract_fusion.9
  211.8 1.2 multiply_subtract_fusion.9
  214.8 1.2 multiply_subtract_fusion.9
  222.2 24.1 %while.55 = (s32[]{:T(128)}, f32[2,8]{1,0:T(2,128)S(1)}, f32[8,2,8]{2,1,0:T(2,128)S(1)}, f32[8,2]{1,0:T(8,128)S(1)}, s32[8]{0:T(128)S(1)}, /*index=5*/s32[]{:T(128)}, s32[]{:T(128)}) while((s32[]{:T(128)}, f32[2,8]{1,0:T(2,128)S(1)}, f32[8,2,8]{2,1,0:T(2,128)S(1)}, f32[8,2]{1,0:T(8,128)S(1)}, s32[8]{0:T(128)S(1)}, ...), condition=%wide.region_5.6_spmd.clone.clone, body=%wide.region_4.5_spmd.clone.clone.sunk | while | flops 123 | bytes 3535 | solution.py:137
  246.9 6.0 %collective-permute-done.7 = f32[1,2,16,256]{3,2,1,0:T(8,128)S(1)} collective-permute-done((f32[1,2,16,256]{3,2,1,0:T(8,128)S(1)}, f32[1,2,16,256]{3,2,1,0:T(8,128)S(1)}, u32[]{:S(2)}, u32[]{:S(2)}) %collective-permute-start.7) | collective-permute-done | bytes 32800 | tf_op jit(solution)/shard_map/ppermute | solution.py:143
  252.9 6.6 %collective-permute-done.8 = f32[1,2,16,256]{3,2,1,0:T(8,128)S(1)} collective-permute-done((f32[1,2,16,256]{3,2,1,0:T(8,128)S(1)}, f32[1,2,16,256]{3,2,1,0:T(8,128)S(1)}, u32[]{:S(2)}, u32[]{:S(2)}) %collective-permute-start.8) | collective-permute-done | bytes 32800 | tf_op jit(solution)/shard_map/ppermute | solution.py:143
  261.1 1.4 multiply_subtract_fusion.5
  262.5 30.7 %all-gather = f32[16,16,256]{2,1,0:T(8,128)S(1)} all-gather(f32[2,16,256]{2,1,0:T(8,128)S(1)} %pad_maximum_fusion.6), channel_id=2, replica_groups=mesh['gx'=8,'gy'=4] {'gx'}, dimensions={0}, use_global_device_ids=true | all-gather | bytes 294912 | tf_op jit(solution)/shard_map/all_gather | solution.py:168
  294.5 1.2 subtract_bitcast_fusion
  295.7 1.2 add_bitcast_fusion
  298.6 1.5 fusion.9
  (305 shorter events, 68.6 us)
Async XLA Ops:
  3.9 168.5 %collective-permute-start = (f32[2,32,16,1]{3,2,1,0:T(8,128)S(1)}, f32[2,32,16,1]{3,2,1,0:T(8,128)}, u32[]{:S(2)}, u32[]{:S(2)}) collective-permute-start(f32[2,32,16,1]{3,2,1,0:T(8,128)S(1)} %get-tuple-element.455), channel_id=1, source_target_pairs={{1,0},{2,1},{3,2},{5,4},{6,5},{7,6},{9,8},{10,9},{11,10},{13,12},{... | collective-permute-start | bytes 12296 | tf_op jit(solution)/shard_map/ppermute | solution.py:18
  5.2 167.2 %collective-permute-start.1 = (f32[2,32,16,1]{3,2,1,0:T(8,128)S(1)}, f32[2,32,16,1]{3,2,1,0:T(8,128)}, u32[]{:S(2)}, u32[]{:S(2)}) collective-permute-start(f32[2,32,16,1]{3,2,1,0:T(8,128)S(1)} %get-tuple-element.456), channel_id=1, source_target_pairs={{0,1},{1,2},{2,3},{4,5},{5,6},{6,7},{8,9},{9,10},{10,11},{12,13},{... | collective-permute-start | bytes 12296 | tf_op jit(solution)/shard_map/ppermute | solution.py:17
  9.0 0.7 copy-start
  9.0 0.7 copy-start.1
  9.0 0.7 copy-start.3
  174.6 0.8 copy-start.2
  176.7 8.0 %collective-permute-start.2 = (f32[1,2,16,256]{3,2,1,0:T(8,128)S(1)}, f32[1,2,16,256]{3,2,1,0:T(8,128)S(1)}, u32[]{:S(2)}, u32[]{:S(2)}) collective-permute-start(f32[1,2,16,256]{3,2,1,0:T(8,128)S(1)} %fusion.37), channel_id=1, source_target_pairs={{0,4},{4,8},{8,12},{12,16},{16,20},{20,24},{24,28},{28,0},{1,5},{5... | collective-permute-start | bytes 98312 | tf_op jit(solution)/shard_map/ppermute | solution.py:143
  184.7 6.6 %collective-permute-start.3 = (f32[1,2,16,256]{3,2,1,0:T(8,128)S(1)}, f32[1,2,16,256]{3,2,1,0:T(8,128)S(1)}, u32[]{:S(2)}, u32[]{:S(2)}) collective-permute-start(f32[1,2,16,256]{3,2,1,0:T(8,128)S(1)} %collective-permute-done.2), channel_id=1, source_target_pairs={{0,4},{4,8},{8,12},{12,16},{16,20},{20,24},{24,28},{28,0},{1,5},{5... | collective-permute-start | bytes 98312 | tf_op jit(solution)/shard_map/ppermute | solution.py:143
  191.3 6.6 %collective-permute-start.4 = (f32[1,2,16,256]{3,2,1,0:T(8,128)S(1)}, f32[1,2,16,256]{3,2,1,0:T(8,128)S(1)}, u32[]{:S(2)}, u32[]{:S(2)}) collective-permute-start(f32[1,2,16,256]{3,2,1,0:T(8,128)S(1)} %collective-permute-done.3), channel_id=1, source_target_pairs={{0,4},{4,8},{8,12},{12,16},{16,20},{20,24},{24,28},{28,0},{1,5},{5... | collective-permute-start | bytes 98312 | tf_op jit(solution)/shard_map/ppermute | solution.py:143
  198.0 24.1 %collective-permute-start.5 = (f32[1,2,16,256]{3,2,1,0:T(8,128)S(1)}, f32[1,2,16,256]{3,2,1,0:T(8,128)S(1)}, u32[]{:S(2)}, u32[]{:S(2)}) collective-permute-start(f32[1,2,16,256]{3,2,1,0:T(8,128)S(1)} %collective-permute-done.4), channel_id=1, source_target_pairs={{0,4},{4,8},{8,12},{12,16},{16,20},{20,24},{24,28},{28,0},{1,5},{5... | collective-permute-start | bytes 98312 | tf_op jit(solution)/shard_map/ppermute | solution.py:143
  222.1 24.2 %collective-permute-start.6 = (f32[1,2,16,256]{3,2,1,0:T(8,128)S(1)}, f32[1,2,16,256]{3,2,1,0:T(8,128)S(1)}, u32[]{:S(2)}, u32[]{:S(2)}) collective-permute-start(f32[1,2,16,256]{3,2,1,0:T(8,128)S(1)} %collective-permute-done.5), channel_id=1, source_target_pairs={{0,4},{4,8},{8,12},{12,16},{16,20},{20,24},{24,28},{28,0},{1,5},{5... | collective-permute-start | bytes 98312 | tf_op jit(solution)/shard_map/ppermute | solution.py:143
  246.2 6.7 %collective-permute-start.7 = (f32[1,2,16,256]{3,2,1,0:T(8,128)S(1)}, f32[1,2,16,256]{3,2,1,0:T(8,128)S(1)}, u32[]{:S(2)}, u32[]{:S(2)}) collective-permute-start(f32[1,2,16,256]{3,2,1,0:T(8,128)S(1)} %collective-permute-done.6), channel_id=1, source_target_pairs={{0,4},{4,8},{8,12},{12,16},{16,20},{20,24},{24,28},{28,0},{1,5},{5... | collective-permute-start | bytes 98312 | tf_op jit(solution)/shard_map/ppermute | solution.py:143
  252.9 6.6 %collective-permute-start.8 = (f32[1,2,16,256]{3,2,1,0:T(8,128)S(1)}, f32[1,2,16,256]{3,2,1,0:T(8,128)S(1)}, u32[]{:S(2)}, u32[]{:S(2)}) collective-permute-start(f32[1,2,16,256]{3,2,1,0:T(8,128)S(1)} %collective-permute-done.7), channel_id=1, source_target_pairs={{0,4},{4,8},{8,12},{12,16},{16,20},{20,24},{24,28},{28,0},{1,5},{5... | collective-permute-start | bytes 98312 | tf_op jit(solution)/shard_map/ppermute | solution.py:143
  261.0 37.1 %copy-start.6 = (f32[32]{0:T(128)S(1)}, f32[32]{0:T(128)}, u32[]{:S(2)}) copy-start(f32[32]{0:T(128)} %constant.176) | copy-start | bytes 388
  261.1 37.1 %copy-start.7 = (f32[32]{0:T(128)S(1)}, f32[32]{0:T(128)}, u32[]{:S(2)}) copy-start(f32[32]{0:T(128)} %constant.174) | copy-start | bytes 388
  293.6 4.8 %copy-start.4 = (f32[32]{0:T(128)S(1)}, f32[32]{0:T(128)}, u32[]{:S(2)}) copy-start(f32[32]{0:T(128)} %constant.172) | copy-start | bytes 388
  293.6 4.8 %copy-start.5 = (f32[32]{0:T(128)S(1)}, f32[32]{0:T(128)}, u32[]{:S(2)}) copy-start(f32[32]{0:T(128)} %constant.153) | copy-start | bytes 388
